TPU v7x, 32 devices: a whole 2x2x4 slice. The times are simulated.
32 devices in a mesh: grp: 2 (over x), blk: 16 (over z, y, core).
Axes of the slice: x: 2, y: 2, z: 4, core: 2. Of those that a mesh axis runs over, the one named last changes fastest.
Arguments:
- sketch: bfloat16 [256, 131072], P(None, 'blk'), may hold values from -3 to 3
- leaf_maps: bfloat16 [2, 16, 256, 256], P('grp', 'blk')
- mix_maps: bfloat16 [2, 64, 16, 16], P('grp', 'blk')
Outputs:
- sketch_update: bfloat16 [256, 131072], P('grp', 'blk')
All inputs are finite; a program needn't handle non-finite values.
Results may differ from a plain program's by a relative error of at most 0.015.
Values may be sent and summed in bfloat16 or wider, within the bound.
A program may use at most 64 MiB of HBM per device.

v0:
```python
import functools

import jax
import jax.numpy as jnp
from jax import lax
from jax.experimental import pallas as pl
from jax.experimental.pallas import tpu as pltpu
from jax.sharding import PartitionSpec as P

MESH = pl.DeviceIdType.MESH
TILE = 16
LANES = 128


def chunk_rows(own_cols):
    left, sizes = own_cols, []
    for size in CHUNKS:
        if left >= size:
            sizes.append(size)
            left -= size
    while left > 0:
        sizes.append(min(left, 2 * TILE))
        left -= sizes[-1]
    return sizes


CHUNKS = (16,16,32,64)


def chain_kernel(
    groups, blocks, sizes, sketch_ref, leaf_in, mix_in, out_ref,
    x_vm, send, recv, half, leaf_all, mix_vm, mix_all, weights,
    x_sem, send_sem, recv_sem, own_sem, leaf_send, leaf_recv, mix_send, mix_recv, go_sem,
):
    grp = lax.axis_index("grp")
    blk = lax.axis_index("blk")
    own_cols, row_len = x_vm.shape
    sub = leaf_in.shape[0] // 2
    leaves = row_len // sub
    low = leaves // blocks
    wide = low * sub
    starts = [sum(sizes[:i]) for i in range(len(sizes))]
    big = blocks * TILE

    barrier = pltpu.get_barrier_semaphore()

    def greet(**where):
        pl.semaphore_signal(barrier, inc=1, device_id=where, device_id_type=MESH)

    @pl.when(grp == 0)
    def _():
        for step in range(blocks):
            greet(grp=1, blk=lax.rem(blk + step, blocks))
        for other in range(2, groups):
            greet(grp=other, blk=blk)

    @pl.when(grp > 0)
    def _():
        for step in range(1, groups):
            greet(grp=lax.rem(grp + step, groups), blk=blk)
        for step in range(1, blocks):
            greet(grp=grp, blk=lax.rem(blk + step, blocks))

    own_mix = pltpu.make_async_copy(mix_in, mix_vm, own_sem.at[0])
    own_leaf = pltpu.make_async_copy(leaf_in, leaf_all.at[grp], own_sem.at[1])
    own_mix.start()
    own_leaf.start()

    def load(chunk):
        rows = pl.ds(pl.multiple_of(grp * own_cols + starts[chunk], TILE), sizes[chunk])
        return pltpu.make_async_copy(
            sketch_ref.at[rows, :], x_vm.at[pl.ds(starts[chunk], sizes[chunk]), :], x_sem.at[chunk])

    for chunk in range(len(sizes)):
        load(chunk).start()

    own_mix.wait()
    pick = (
        lax.broadcasted_iota(jnp.int32, (blocks, blocks), 0)
        == lax.broadcasted_iota(jnp.int32, (blocks, blocks), 1)
    ).astype(jnp.bfloat16)
    mix_all[grp] = jnp.zeros(mix_all.shape[1:], jnp.bfloat16)
    mix_all[grp, :, pl.ds(0, low * blocks)] = lax.dot_general(
        pick, mix_vm[...], (((1,), (1,)), ((), ())), preferred_element_type=jnp.float32
    ).astype(jnp.bfloat16)
    def factor_copies(target, owner):
        where = {"grp": target}
        return (
            pltpu.make_async_remote_copy(
                mix_all.at[owner], mix_all.at[owner], mix_send.at[target], mix_recv.at[owner],
                device_id=where, device_id_type=MESH),
            pltpu.make_async_remote_copy(
                leaf_in, leaf_all.at[owner], leaf_send.at[target], leaf_recv.at[owner],
                device_id=where, device_id_type=MESH),
        )

    def send_factors():
        for step in range(1, groups):
            for copy in factor_copies(lax.rem(grp + step, groups), grp):
                copy.start()

    @pl.when(grp == 0)
    def _():
        pl.semaphore_wait(barrier, groups - 1)
        send_factors()

    @pl.when(grp == 1)
    def _():
        pl.semaphore_wait(barrier, 2 * blocks - 1 + groups - 2)
        pl.semaphore_signal(go_sem, inc=1, device_id={"grp": 0}, device_id_type=MESH)

    @pl.when(grp > 1)
    def _():
        pl.semaphore_wait(barrier, blocks - 1 + groups - 1)

    spread = (
        lax.broadcasted_iota(jnp.int32, (big, blocks), 0) // TILE
        == lax.broadcasted_iota(jnp.int32, (big, blocks), 1)
    ).astype(jnp.bfloat16)
    same = (
        lax.broadcasted_iota(jnp.int32, (big, big), 0) % TILE
        == lax.broadcasted_iota(jnp.int32, (big, big), 1) % TILE
    )
    nums = (((1,), (1,)), ((), ()))
    width = mix_all.shape[2]

    def build_weights(section):
        for l in range(low):
            chosen = (
                lax.broadcasted_iota(jnp.int32, (big, width), 0) // TILE + l * blocks
                == lax.broadcasted_iota(jnp.int32, (big, width), 1)
            ).astype(jnp.bfloat16)
            tall = lax.dot_general(
                chosen, mix_all[section], nums, preferred_element_type=jnp.float32
            ).astype(jnp.bfloat16)
            full = lax.dot_general(tall, spread, nums, preferred_element_type=jnp.float32)
            weights[l] = jnp.where(same, full, 0.0).astype(jnp.bfloat16)

    def compute(section, start, rows):
        unit = pl.ds(start, rows)
        tiles = rows // TILE

        def piece(leaf):
            if section == 0:
                return x_vm[unit, pl.ds(leaf * sub, sub)]
            return recv[section - 1, leaf // low, unit, pl.ds(leaf % low * sub, sub)]

        leaf_map = leaf_all[section]
        per = min(leaves // 2, max(1, 256 // rows))
        for first in range(0, leaves // 2, per):
            lhs = jnp.concatenate(
                [jnp.concatenate([piece(2 * m), piece(2 * m + 1)], axis=1)
                 for m in range(first, first + per)], axis=0)
            product = jnp.dot(
                lhs, leaf_map, preferred_element_type=jnp.float32).astype(jnp.bfloat16)
            for i in range(per):
                for j in range(2):
                    half[2 * (first + i) + j, pl.ds(0, rows), :] = product[
                        i * rows:(i + 1) * rows, j * sub:(j + 1) * sub]

        for l in range(low):
            rhs = jnp.concatenate(
                [jnp.concatenate(
                    [half[k * low + l, pl.ds(t * TILE, TILE), :] for t in range(tiles)], axis=1)
                 for k in range(blocks)], axis=0)
            mixed = jnp.dot(
                weights[l], rhs, preferred_element_type=jnp.float32).astype(jnp.bfloat16)
            for h in range(blocks):
                for t in range(tiles):
                    send[section, h, pl.ds(start + t * TILE, TILE), pl.ds(l * sub, sub)] = mixed[
                        h * TILE:(h + 1) * TILE, t * sub:(t + 1) * sub]

    order = list(range(1, blocks))

    for section in range(groups):
        @pl.when(grp != section)
        def _():
            factor_copies(section, section)[0].wait_recv()

        build_weights(section)

        @pl.when(grp != section)
        def _():
            factor_copies(section, section)[1].wait_recv()

        @pl.when(grp == section)
        def _():
            own_leaf.wait()

        for chunk, (start, rows) in enumerate(zip(starts, sizes)):
            span = pl.ds(start, rows)
            if section == 0:
                load(chunk).wait()
            else:
                arrived = recv.at[section - 1, :, span, :]
                pltpu.make_async_copy(arrived, arrived, recv_sem.at[section - 1, chunk]).wait()

            unit = half.shape[1]
            if rows <= unit:
                compute(section, start, rows)
            else:
                @pl.loop(0, rows // unit)
                def _(i):
                    compute(section, pl.multiple_of(start + i * unit, TILE), unit)

            if section == 0 and chunk == 0:
                @pl.when(grp == 0)
                def _():
                    pl.semaphore_wait(go_sem, 1)

                @pl.when(grp > 0)
                def _():
                    send_factors()

            if section == groups - 1:
                place = out_ref.at[span, pl.ds(pl.multiple_of(blk * wide, sub), wide)]
            else:
                place = recv.at[section, blk, span, :]
            for step in order:
                target = lax.rem(blk + step, blocks)
                pltpu.make_async_remote_copy(
                    send.at[section, target, span, :], place,
                    send_sem.at[section, chunk], recv_sem.at[section, chunk],
                    device_id={"blk": target}, device_id_type=MESH).start()
            pltpu.make_async_copy(
                send.at[section, blk, span, :], place, recv_sem.at[section, chunk]).start()

    for step in range(1, groups):
        for copy in factor_copies(lax.rem(grp + step, groups), grp):
            copy.wait_send()
    for chunk, (start, rows) in enumerate(zip(starts, sizes)):
        span = pl.ds(start, rows)
        for section in range(groups):
            left = send.at[section, pl.ds(0, blocks - 1), span, :]
            pltpu.make_async_copy(left, left, send_sem.at[section, chunk]).wait()
        arrived = out_ref.at[span, :]
        pltpu.make_async_copy(arrived, arrived, recv_sem.at[groups - 1, chunk]).wait()


def on_device(sketch, leaf_maps, mix_maps):
    groups, blocks = lax.axis_size("grp"), lax.axis_size("blk")
    total_cols, rows_dev = sketch.shape
    own_cols = total_cols // groups
    pair = leaf_maps.shape[2]
    sub = pair // 2
    leaves = rows_dev // sub
    low = leaves // blocks
    sizes = chunk_rows(own_cols)
    big = blocks * TILE
    width = -(-low * blocks // LANES) * LANES
    in_hbm = pl.BlockSpec(memory_space=pltpu.HBM)
    dma = pltpu.SemaphoreType.DMA
    bf16 = jnp.bfloat16
    return pl.pallas_call(
        functools.partial(chain_kernel, groups, blocks, sizes),
        out_shape=jax.ShapeDtypeStruct((own_cols, rows_dev), bf16),
        in_specs=[in_hbm, in_hbm, in_hbm],
        out_specs=pl.BlockSpec(memory_space=pl.ANY),
        scratch_shapes=[
            pltpu.VMEM((own_cols, rows_dev), bf16),
            pltpu.VMEM((groups, blocks, own_cols, low * sub), bf16),
            pltpu.VMEM((groups - 1, blocks, own_cols, low * sub), bf16),
            pltpu.VMEM((leaves, 2 * TILE, sub), bf16),
            pltpu.VMEM((groups, pair, pair), bf16),
            pltpu.VMEM((low * blocks, blocks), bf16),
            pltpu.VMEM((groups, blocks, width), bf16),
            pltpu.VMEM((low, big, big), bf16),
            dma((len(sizes),)),
            dma((groups, len(sizes))),
            dma((groups, len(sizes))),
            dma((2,)),
            dma((groups,)), dma((groups,)), dma((groups,)), dma((groups,)),
            pltpu.SemaphoreType.REGULAR,
        ],
        compiler_params=pltpu.CompilerParams(
            collective_id=0, has_side_effects=True, vmem_limit_bytes=48 * 1024 * 1024),
    )(sketch, leaf_maps.reshape(pair, pair), mix_maps.reshape(low * blocks, blocks))


def solution(mesh):
    placed = (P(None, "blk"), P("grp", "blk", None, None), P("grp", "blk", None, None))
    return jax.shard_map(
        on_device, mesh=mesh, in_specs=placed, out_specs=P("grp", "blk"), check_vma=False
    )
```

profile of v0, /device:TPU:15, one launch (start us, length us, event | category | flops | bytes accessed | tf_op | source)
XLA Modules:
  0.0 100.5 jit_solution(1152516679166331870)
XLA Ops:
  0.0 0.0 copy-start
  0.0 0.9 copy-done
  0.9 0.0 copy-start.1
  0.9 0.7 copy-done.1
  1.6 97.6 %shard_map.37 = bf16[128,8192]{1,0:T(8,128)(2,1)S(1)} custom-call(bf16[256,8192]{1,0:T(8,128)(2,1)} %sketch_ref.1, bf16[256,256]{1,0:T(8,128)(2,1)S(1)} %bitcast.2, bf16[64,16]{1,0:T(8,128)(2,1)S(1)} %bitcast.3), custom_call_target="tpu_custom_call" | custom-call | tf_op jit(solution)/shard_map/pallas_call | solution.py:254
  99.2 1.3 %copy.5 = bf16[128,8192]{1,0:T(8,128)(2,1)} copy(bf16[128,8192]{1,0:T(8,128)(2,1)S(1)} %shard_map.37) | data formatting | bytes 4194304
Async XLA Ops:
  0.0 0.9 copy-start
  0.9 0.7 copy-start.1
where the time goes:
time: 101 us
  Pallas kernels  97.6 us (97%)
  local copies, waits for them, and re-layouts  2.94 us (3%)
    pallas_call x1, Pallas kernels, on_device(): pl.pallas_call(functools.partial(chain_kernel, groups, blocks, sizes), ou...  97.6 us
    unnamed x5, local copies, waits for them, and re-layouts  2.94 us

commit v1 on v0

--- a/solution.py
+++ b/solution.py
@@ -35,7 +35,7 @@
     grp = lax.axis_index("grp")
     blk = lax.axis_index("blk")
     own_cols, row_len = x_vm.shape
-    sub = leaf_in.shape[0] // 2
+    sub = leaf_in.shape[2] // 2
     leaves = row_len // sub
     low = leaves // blocks
     wide = low * sub
@@ -61,8 +61,8 @@
         for step in range(1, blocks):
             greet(grp=grp, blk=lax.rem(blk + step, blocks))
 
-    own_mix = pltpu.make_async_copy(mix_in, mix_vm, own_sem.at[0])
-    own_leaf = pltpu.make_async_copy(leaf_in, leaf_all.at[grp], own_sem.at[1])
+    own_mix = pltpu.make_async_copy(mix_in.at[0], mix_vm, own_sem.at[0])
+    own_leaf = pltpu.make_async_copy(leaf_in.at[0, 0], leaf_all.at[grp], own_sem.at[1])
     own_mix.start()
     own_leaf.start()
 
@@ -81,7 +81,8 @@
     ).astype(jnp.bfloat16)
     mix_all[grp] = jnp.zeros(mix_all.shape[1:], jnp.bfloat16)
     mix_all[grp, :, pl.ds(0, low * blocks)] = lax.dot_general(
-        pick, mix_vm[...], (((1,), (1,)), ((), ())), preferred_element_type=jnp.float32
+        pick, mix_vm[...].reshape(low * blocks, blocks), (((1,), (1,)), ((), ())),
+        preferred_element_type=jnp.float32
     ).astype(jnp.bfloat16)
     def factor_copies(target, owner):
         where = {"grp": target}
@@ -90,7 +91,7 @@
                 mix_all.at[owner], mix_all.at[owner], mix_send.at[target], mix_recv.at[owner],
                 device_id=where, device_id_type=MESH),
             pltpu.make_async_remote_copy(
-                leaf_in, leaf_all.at[owner], leaf_send.at[target], leaf_recv.at[owner],
+                leaf_in.at[0, 0], leaf_all.at[owner], leaf_send.at[target], leaf_recv.at[owner],
                 device_id=where, device_id_type=MESH),
         )
 
@@ -262,7 +263,7 @@
             pltpu.VMEM((groups - 1, blocks, own_cols, low * sub), bf16),
             pltpu.VMEM((leaves, 2 * TILE, sub), bf16),
             pltpu.VMEM((groups, pair, pair), bf16),
-            pltpu.VMEM((low * blocks, blocks), bf16),
+            pltpu.VMEM((low, blocks, blocks), bf16),
             pltpu.VMEM((groups, blocks, width), bf16),
             pltpu.VMEM((low, big, big), bf16),
             dma((len(sizes),)),
@@ -274,7 +275,7 @@
         ],
         compiler_params=pltpu.CompilerParams(
             collective_id=0, has_side_effects=True, vmem_limit_bytes=48 * 1024 * 1024),
-    )(sketch, leaf_maps.reshape(pair, pair), mix_maps.reshape(low * blocks, blocks))
+    )(sketch, pltpu.with_memory_space_constraint(leaf_maps, pltpu.HBM), pltpu.with_memory_space_constraint(mix_maps, pltpu.HBM))
 
 
 def solution(mesh):

time: 101 us -> 99.2 us (0.982)
  local copies, waits for them, and re-layouts: 2.94 us -> 1.32 us
    unnamed x5 -> x1, local copies, waits for them, and re-layouts: 2.94 us -> 1.32 us
where the time goes in v1:
time: 99.2 us; the launch traced here: 99.1 us
  Pallas kernels  97.8 us (99%)
  local copies, waits for them, and re-layouts  1.32 us (1%)
    pallas_call x1, Pallas kernels, on_device(): pl.pallas_call(functools.partial(chain_kernel, groups, blocks, sizes), ou...  97.8 us

profile of v1, /device:TPU:15, one launch (start us, length us, event | category | flops | bytes accessed | tf_op | source)
XLA Modules:
  0.0 99.1 jit_solution(5160998379037230528)
XLA Ops:
  0.0 97.8 %shard_map.37 = bf16[128,8192]{1,0:T(8,128)(2,1)S(1)} custom-call(bf16[256,8192]{1,0:T(8,128)(2,1)} %sketch_ref.1, bf16[1,1,256,256]{3,2,1,0:T(8,128)(2,1)} %leaf_in.1, bf16[1,4,16,16]{3,2,1,0:T(8,128)(2,1)} %mix_in.1), custom_call_target="tpu_custom_call" | custom-call | tf_op jit(solution)/shard_map/pallas_call | solution.py:255
  97.8 1.3 %copy.5 = bf16[128,8192]{1,0:T(8,128)(2,1)} copy(bf16[128,8192]{1,0:T(8,128)(2,1)S(1)} %shard_map.37) | data formatting | bytes 4194304

commit v2 on v1

v2 whole, which is shorter than its diff:
```python
import functools

import jax
import jax.numpy as jnp
from jax import lax
from jax.experimental import pallas as pl
from jax.experimental.pallas import tpu as pltpu
from jax.sharding import PartitionSpec as P

MESH = pl.DeviceIdType.MESH
TILE = 16
LANES = 128
CHUNKS = (16, 16, 32, 64)


def chunk_rows(own_cols):
    left, sizes = own_cols, []
    for size in CHUNKS:
        if left >= size:
            sizes.append(size)
            left -= size
    while left > 0:
        sizes.append(min(left, 2 * TILE))
        left -= sizes[-1]
    return sizes


def chain_kernel(
    groups, blocks, own_cols, sizes, sketch_ref, leaf_in, mix_in, out_ref,
    x_vm, send, recv, half, leaf_all, mix_vm, mix_all, weights, lent,
    x_sem, send_sem, recv_sem, own_sem, leaf_send, leaf_recv, mix_send, mix_recv, lent_sem,
    near_sem, far_sem, all_sem,
):
    grp = lax.axis_index("grp")
    blk = lax.axis_index("blk")
    row_len = x_vm.shape[1]
    sub = leaf_in.shape[2] // 2
    leaves = row_len // sub
    low = leaves // blocks
    wide = low * sub
    starts = [sum(sizes[:i]) for i in range(len(sizes))]
    big = blocks * TILE
    far = blocks * 3 // 4
    width = mix_all.shape[2]
    parts = [pl.ds(i * sub, sub) for i in range(2)]
    split = low % 2 == 0

    lend = split and groups == 2 and len(sizes) > 1
    given = low - 1
    middle = blocks // 2
    lent_to = ((far, blocks), (0, middle))

    def each_half(act):
        for upper in range(2):
            @pl.when((blk >= middle) == bool(upper))
            def _():
                act(*lent_to[upper])

    barrier = pltpu.get_barrier_semaphore()
    for step in range(1, groups):
        pl.semaphore_signal(
            barrier, inc=1, device_id={"grp": lax.rem(grp + step, groups)}, device_id_type=MESH)

    @pl.loop(blk + 1, blocks)
    def _(other):
        pl.semaphore_signal(barrier, inc=1, device_id={"blk": other}, device_id_type=MESH)

    own_mix = pltpu.make_async_copy(mix_in.at[0], mix_vm, own_sem.at[0])
    own_leaf = pltpu.make_async_copy(leaf_in.at[0, 0], leaf_all.at[grp], own_sem.at[1])

    def load(chunk):
        rows = pl.ds(pl.multiple_of(grp * own_cols + starts[chunk], TILE), sizes[chunk])
        return pltpu.make_async_copy(
            sketch_ref.at[rows, :], x_vm.at[pl.ds(starts[chunk], sizes[chunk]), :], x_sem.at[chunk])

    lent_load = pltpu.make_async_copy(
        sketch_ref.at[pl.ds(own_cols + starts[0], sizes[0]), :],
        x_vm.at[pl.ds(own_cols, sizes[0]), :], x_sem.at[len(sizes)])

    own_mix.start()
    own_leaf.start()
    for chunk in range(len(sizes)):
        load(chunk).start()
    if lend:
        @pl.when(grp == 0)
        def _():
            lent_load.start()

    def mix_copy(target, owner):
        return pltpu.make_async_remote_copy(
            mix_all.at[owner], mix_all.at[owner], mix_send.at[target], mix_recv.at[owner],
            device_id={"grp": target}, device_id_type=MESH)

    def leaf_copy(target, owner, part):
        return pltpu.make_async_remote_copy(
            leaf_all.at[owner, :, parts[part]], leaf_all.at[owner, :, parts[part]],
            leaf_send.at[target, part], leaf_recv.at[owner, part],
            device_id={"grp": target}, device_id_type=MESH)

    def send_factors():
        own_leaf.wait()
        for step in range(1, groups):
            target = lax.rem(grp + step, groups)
            mix_copy(target, grp).start()
            for part in range(2):
                leaf_copy(target, grp, part).start()

    spread = (
        lax.broadcasted_iota(jnp.int32, (big, blocks), 0) // TILE
        == lax.broadcasted_iota(jnp.int32, (big, blocks), 1)
    ).astype(jnp.bfloat16)
    same = (
        lax.broadcasted_iota(jnp.int32, (big, big), 0) % TILE
        == lax.broadcasted_iota(jnp.int32, (big, big), 1) % TILE
    )
    nums = (((1,), (1,)), ((), ()))

    def own_mixing():
        own_mix.wait()
        pick = (
            lax.broadcasted_iota(jnp.int32, (blocks, blocks), 0)
            == lax.broadcasted_iota(jnp.int32, (blocks, blocks), 1)
        ).astype(jnp.bfloat16)
        mix_all[grp] = jnp.zeros(mix_all.shape[1:], jnp.bfloat16)
        mix_all[grp, :, pl.ds(0, low * blocks)] = lax.dot_general(
            pick, mix_vm[...].reshape(low * blocks, blocks), nums, preferred_element_type=jnp.float32
        ).astype(jnp.bfloat16)

    def build_weights(section, inner):
        for l in inner:
            chosen = (
                lax.broadcasted_iota(jnp.int32, (big, width), 0) // TILE + l * blocks
                == lax.broadcasted_iota(jnp.int32, (big, width), 1)
            ).astype(jnp.bfloat16)
            tall = lax.dot_general(
                chosen, mix_all[section], nums, preferred_element_type=jnp.float32
            ).astype(jnp.bfloat16)
            full = lax.dot_general(tall, spread, nums, preferred_element_type=jnp.float32)
            weights[l] = jnp.where(same, full, 0.0).astype(jnp.bfloat16)

    def leaf_step(section, start, rows, part=None):
        unit = pl.ds(start, rows)

        def piece(leaf):
            if section == 0:
                return x_vm[unit, pl.ds(leaf * sub, sub)]
            return recv[section - 1, leaf // low, unit, pl.ds(leaf % low * sub, sub)]

        leaf_map = leaf_all[section] if part is None else leaf_all[section, :, parts[part]]
        per = min(leaves // 2, max(1, 256 // rows))
        for first in range(0, leaves // 2, per):
            lhs = jnp.concatenate(
                [jnp.concatenate([piece(2 * m), piece(2 * m + 1)], axis=1)
                 for m in range(first, first + per)], axis=0)
            product = jnp.dot(
                lhs, leaf_map, preferred_element_type=jnp.float32).astype(jnp.bfloat16)
            for i in range(per):
                for j in (range(2) if part is None else (part,)):
                    at = j * sub if part is None else 0
                    half[2 * (first + i) + j, pl.ds(0, rows), :] = product[
                        i * rows:(i + 1) * rows, at:at + sub]

    def mix_step(section, start, rows, inner, goal=None):
        tiles = rows // TILE
        for l in inner:
            rhs = jnp.concatenate(
                [jnp.concatenate(
                    [half[k * low + l, pl.ds(t * TILE, TILE), :] for t in range(tiles)], axis=1)
                 for k in range(blocks)], axis=0)
            mixed = jnp.dot(
                weights[l], rhs, preferred_element_type=jnp.float32).astype(jnp.bfloat16)
            for h in range(blocks):
                for t in range(tiles):
                    tile = mixed[h * TILE:(h + 1) * TILE, t * sub:(t + 1) * sub]
                    if goal is not None:
                        goal[h, pl.ds(t * TILE, TILE), :] = tile
                    else:
                        send[section, h, pl.ds(start + t * TILE, TILE), pl.ds(l * sub, sub)] = tile

    def compute(section, start, rows):
        leaf_step(section, start, rows)
        mix_step(section, start, rows, range(low))

    def place(section, span):
        if section == groups - 1:
            return out_ref.at[span, pl.ds(pl.multiple_of(blk * wide, sub), wide)]
        return recv.at[section, blk, span, :]

    def push(section, chunk, target, inner=None):
        span = pl.ds(starts[chunk], sizes[chunk])
        source, goal = send.at[section, target, span, :], place(section, span)
        if inner is not None:
            source, goal = (ref.at[:, pl.ds(inner * sub, sub)] for ref in (source, goal))
        pltpu.make_async_remote_copy(
            source, goal, send_sem.at[section, chunk], recv_sem.at[section, chunk],
            device_id={"blk": target}, device_id_type=MESH).start()

    def keep(section, chunk):
        span = pl.ds(starts[chunk], sizes[chunk])
        pltpu.make_async_copy(
            send.at[section, blk, span, :], place(section, span), recv_sem.at[section, chunk]).start()

    def push_some(section, chunk, first, last, inner=None):
        @pl.loop(first, last)
        def _(target):
            push(section, chunk, target, inner)

    def push_all(section, chunk, inner=None):
        for step in range(1, blocks):
            push(section, chunk, lax.rem(blk + step, blocks), inner)

    def meet(of_near, of_far):
        if of_near:
            @pl.when(blk < far - 1)
            def _():
                pl.semaphore_wait(near_sem, far - 1 - blk)
        if of_far:
            @pl.when(blk < blocks - 1)
            def _():
                pl.semaphore_wait(far_sem, blocks - lax.max(far, blk + 1))

    def first_chunk():
        start, rows = starts[0], sizes[0]
        load(0).wait()

        @pl.when(grp == 0)
        def _():
            leaf_step(0, start, rows)
            for l in range(low):
                if l > 0:
                    build_weights(0, [l])
                mix_step(0, start, rows, [l])
                push_some(0, 0, 0, blk, l)
            keep(0, 0)
            meet(True, False)
            push_some(0, 0, blk + 1, far)
            meet(False, True)
            push_some(0, 0, lax.max(far, blk + 1), blocks)

        @pl.when(grp > 0)
        def _():

            def share(l):
                mix_step(0, start, rows, [l])
                if lend and l == given:
                    def rest(first, last):
                        push_some(0, 0, 0, lax.min(blk, first), l)
                        push_some(0, 0, blk + 1, first, l)
                        push_some(0, 0, last, blk, l)
                        push_some(0, 0, lax.max(last, blk + 1), blocks, l)
                    each_half(rest)
                else:
                    push_all(0, 0, l)

            meet(True, True)
            if lend:
                pl.semaphore_signal(all_sem, inc=1, device_id={"grp": 0}, device_id_type=MESH)
            for part in range(2):
                leaf_copy(0, 0, part).wait_recv()
                leaf_step(0, start, rows, part)
                if split:
                    for l in range(part, low, 2):
                        share(l)
            if not split:
                for l in range(low):
                    share(l)
            keep(0, 0)

    lent_cols = pl.ds(given * sub, sub)

    def lent_copy(target):
        return pltpu.make_async_remote_copy(
            lent.at[target], recv.at[0, blk, pl.ds(starts[0], sizes[0]), lent_cols],
            lent_sem, recv_sem.at[0, 0],
            device_id={"grp": 1, "blk": target}, device_id_type=MESH)

    def lent_chunk():
        @pl.when(grp == 0)
        def _():
            lent_load.wait()
            leaf_step(0, own_cols, sizes[0], given % 2)
            mix_step(0, own_cols, sizes[0], [given], lent)
            pl.semaphore_wait(all_sem, 1)

            def start(first, last):
                for step in range(last - first):
                    lent_copy(first + lax.rem(blk + step, last - first)).start()
            each_half(start)

    own_mixing()

    @pl.when(grp == 0)
    def _():
        build_weights(0, [0])

    pl.semaphore_wait(barrier, blk + groups - 1)
    send_factors()

    @pl.loop(0, blk)
    def _(other):
        @pl.when(blk < far)
        def _():
            pl.semaphore_signal(near_sem, inc=1, device_id={"blk": other}, device_id_type=MESH)

        @pl.when(blk >= far)
        def _():
            pl.semaphore_signal(far_sem, inc=1, device_id={"blk": other}, device_id_type=MESH)

    @pl.when(grp > 0)
    def _():
        mix_copy(0, 0).wait_recv()
        build_weights(0, range(low))

    for section in range(groups):
        if section > 0:
            @pl.when(grp != section)
            def _():
                mix_copy(section, section).wait_recv()

            build_weights(section, range(low))

        if section > 0:
            @pl.when(grp != section)
            def _():
                for part in range(2):
                    leaf_copy(section, section, part).wait_recv()

        for chunk, (start, rows) in enumerate(zip(starts, sizes)):
            if section == 0 and chunk == 0:
                first_chunk()
                continue
            if section == 0:
                load(chunk).wait()
            else:
                arrived = recv.at[section - 1, :, pl.ds(start, rows), :]
                pltpu.make_async_copy(arrived, arrived, recv_sem.at[section - 1, chunk]).wait()

            unit = half.shape[1]
            if rows <= unit:
                compute(section, start, rows)
            else:
                @pl.loop(0, rows // unit)
                def _(i):
                    compute(section, pl.multiple_of(start + i * unit, TILE), unit)
            push_all(section, chunk)
            keep(section, chunk)
            if section == 0 and chunk == 1 and lend:
                lent_chunk()

    for step in range(1, groups):
        target = lax.rem(grp + step, groups)
        mix_copy(target, grp).wait_send()
        for part in range(2):
            leaf_copy(target, grp, part).wait_send()
    for chunk, (start, rows) in enumerate(zip(starts, sizes)):
        span = pl.ds(start, rows)
        for section in range(groups):
            left = send.at[section, pl.ds(0, blocks - 1), span, :]
            if lend and section == 0 and chunk == 0:
                @pl.when(grp == 0)
                def _():
                    pltpu.make_async_copy(left, left, send_sem.at[section, chunk]).wait()

                    def sent(first, last):
                        part = lent.at[pl.ds(0, last - first)]
                        pltpu.make_async_copy(part, part, lent_sem).wait()
                    each_half(sent)

                @pl.when(grp > 0)
                def _():
                    def sent(first, last):
                        whole = left.at[:, :, pl.ds(0, given * sub)]
                        part = left.at[pl.ds(0, blocks - 1 - (last - first)), :, lent_cols]
                        for piece in (whole, part):
                            pltpu.make_async_copy(piece, piece, send_sem.at[section, chunk]).wait()
                    each_half(sent)
            else:
                pltpu.make_async_copy(left, left, send_sem.at[section, chunk]).wait()
        arrived = out_ref.at[span, :]
        pltpu.make_async_copy(arrived, arrived, recv_sem.at[groups - 1, chunk]).wait()


def on_device(sketch, leaf_maps, mix_maps):
    groups, blocks = lax.axis_size("grp"), lax.axis_size("blk")
    total_cols, rows_dev = sketch.shape
    own_cols = total_cols // groups
    pair = leaf_maps.shape[2]
    sub = pair // 2
    leaves = rows_dev // sub
    low = leaves // blocks
    sizes = chunk_rows(own_cols)
    big = blocks * TILE
    width = -(-low * blocks // LANES) * LANES
    in_hbm = pl.BlockSpec(memory_space=pltpu.HBM)
    dma = pltpu.SemaphoreType.DMA
    bf16 = jnp.bfloat16
    keep = functools.partial(pltpu.with_memory_space_constraint, memory_space=pltpu.HBM)
    return pl.pallas_call(
        functools.partial(chain_kernel, groups, blocks, own_cols, sizes),
        out_shape=jax.ShapeDtypeStruct((own_cols, rows_dev), bf16),
        in_specs=[in_hbm, in_hbm, in_hbm],
        out_specs=pl.BlockSpec(memory_space=pl.ANY),
        scratch_shapes=[
            pltpu.VMEM((own_cols + sizes[0], rows_dev), bf16),
            pltpu.VMEM((groups, blocks, own_cols, low * sub), bf16),
            pltpu.VMEM((groups - 1, blocks, own_cols, low * sub), bf16),
            pltpu.VMEM((leaves, 2 * TILE, sub), bf16),
            pltpu.VMEM((groups, pair, pair), bf16),
            pltpu.VMEM((low, blocks, blocks), bf16),
            pltpu.VMEM((groups, blocks, width), bf16),
            pltpu.VMEM((low, big, big), bf16),
            pltpu.VMEM((blocks, sizes[0], sub), bf16),
            dma((len(sizes) + 1,)),
            dma((groups, len(sizes))),
            dma((groups, len(sizes))),
            dma((2,)),
            dma((groups, 2)), dma((groups, 2)), dma((groups,)), dma((groups,)), dma,
            pltpu.SemaphoreType.REGULAR, pltpu.SemaphoreType.REGULAR, pltpu.SemaphoreType.REGULAR,
        ],
        compiler_params=pltpu.CompilerParams(
            collective_id=0, has_side_effects=True, vmem_limit_bytes=48 * 1024 * 1024),
    )(sketch, keep(leaf_maps), keep(mix_maps))


def solution(mesh):
    placed = (P(None, "blk"), P("grp", "blk", None, None), P("grp", "blk", None, None))
    return jax.shard_map(
        on_device, mesh=mesh, in_specs=placed, out_specs=P("grp", "blk"), check_vma=False
    )
```

time: 99.2 us -> 97.9 us (0.987)
  Pallas kernels: 97.8 us -> 95.9 us
    pallas_call x1, Pallas kernels: 97.8 us -> 95.9 us  [on_device(): pl.pallas_call(functools.partial(chain_kernel, groups, blocks, own_cols,...]
where the time goes in v2:
time: 97.9 us; the launch traced here: 97.2 us
  Pallas kernels  95.9 us (98%)
  local copies, waits for them, and re-layouts  1.32 us (1%)
    pallas_call x1, Pallas kernels, on_device(): pl.pallas_call(functools.partial(chain_kernel, groups, blocks, own_cols,...  95.9 us

profile of v2, /device:TPU:15, one launch (start us, length us, event | category | flops | bytes accessed | tf_op | source)
XLA Modules:
  0.0 97.2 jit_solution(16193932097203152635)
XLA Ops:
  0.0 95.9 %shard_map.37 = bf16[128,8192]{1,0:T(8,128)(2,1)S(1)} custom-call(bf16[256,8192]{1,0:T(8,128)(2,1)} %sketch_ref.1, bf16[1,1,256,256]{3,2,1,0:T(8,128)(2,1)} %leaf_in.1, bf16[1,4,16,16]{3,2,1,0:T(8,128)(2,1)} %mix_in.1), custom_call_target="tpu_custom_call" | custom-call | tf_op jit(solution)/shard_map/pallas_call | solution.py:398
  95.9 1.3 %copy.5 = bf16[128,8192]{1,0:T(8,128)(2,1)} copy(bf16[128,8192]{1,0:T(8,128)(2,1)S(1)} %shard_map.37) | data formatting | bytes 4194304

commit v3 on v2

--- a/solution.py
+++ b/solution.py
@@ -10,7 +10,7 @@
 MESH = pl.DeviceIdType.MESH
 TILE = 16
 LANES = 128
-CHUNKS = (16, 16, 32, 64)
+CHUNKS = (32, 32, 64)
 
 
 def chunk_rows(own_cols):
@@ -29,7 +29,7 @@
     groups, blocks, own_cols, sizes, sketch_ref, leaf_in, mix_in, out_ref,
     x_vm, send, recv, half, leaf_all, mix_vm, mix_all, weights, lent,
     x_sem, send_sem, recv_sem, own_sem, leaf_send, leaf_recv, mix_send, mix_recv, lent_sem,
-    near_sem, far_sem, all_sem,
+    go_sem, all_sem,
 ):
     grp = lax.axis_index("grp")
     blk = lax.axis_index("blk")
@@ -46,9 +46,10 @@
     split = low % 2 == 0
 
     lend = split and groups == 2 and len(sizes) > 1
+    lent_rows = lent.shape[1]
     given = low - 1
     middle = blocks // 2
-    lent_to = ((far, blocks), (0, middle))
+    lent_to = ((blocks - middle // 4, blocks), (0, middle // 2))
 
     def each_half(act):
         for upper in range(2):
@@ -74,8 +75,8 @@
             sketch_ref.at[rows, :], x_vm.at[pl.ds(starts[chunk], sizes[chunk]), :], x_sem.at[chunk])
 
     lent_load = pltpu.make_async_copy(
-        sketch_ref.at[pl.ds(own_cols + starts[0], sizes[0]), :],
-        x_vm.at[pl.ds(own_cols, sizes[0]), :], x_sem.at[len(sizes)])
+        sketch_ref.at[pl.ds(own_cols, lent_rows), :],
+        x_vm.at[pl.ds(own_cols, lent_rows), :], x_sem.at[len(sizes)])
 
     own_mix.start()
     own_leaf.start()
@@ -97,13 +98,13 @@
             leaf_send.at[target, part], leaf_recv.at[owner, part],
             device_id={"grp": target}, device_id_type=MESH)
 
-    def send_factors():
-        own_leaf.wait()
+    def send_mix():
         for step in range(1, groups):
-            target = lax.rem(grp + step, groups)
-            mix_copy(target, grp).start()
-            for part in range(2):
-                leaf_copy(target, grp, part).start()
+            mix_copy(lax.rem(grp + step, groups), grp).start()
+
+    def send_leaf(part):
+        for step in range(1, groups):
+            leaf_copy(lax.rem(grp + step, groups), grp, part).start()
 
     spread = (
         lax.broadcasted_iota(jnp.int32, (big, blocks), 0) // TILE
@@ -138,7 +139,7 @@
             full = lax.dot_general(tall, spread, nums, preferred_element_type=jnp.float32)
             weights[l] = jnp.where(same, full, 0.0).astype(jnp.bfloat16)
 
-    def leaf_step(section, start, rows, part=None):
+    def leaf_step(section, start, rows, part=None, stage=None):
         unit = pl.ds(start, rows)
 
         def piece(leaf):
@@ -147,17 +148,18 @@
             return recv[section - 1, leaf // low, unit, pl.ds(leaf % low * sub, sub)]
 
         leaf_map = leaf_all[section] if part is None else leaf_all[section, :, parts[part]]
-        per = min(leaves // 2, max(1, 256 // rows))
-        for first in range(0, leaves // 2, per):
+        pairs = range(leaves // 2) if stage is None else range(stage, leaves // 2, low // 2)
+        per = min(len(pairs), max(1, 256 // rows))
+        for first in range(0, len(pairs), per):
             lhs = jnp.concatenate(
                 [jnp.concatenate([piece(2 * m), piece(2 * m + 1)], axis=1)
-                 for m in range(first, first + per)], axis=0)
+                 for m in pairs[first:first + per]], axis=0)
             product = jnp.dot(
                 lhs, leaf_map, preferred_element_type=jnp.float32).astype(jnp.bfloat16)
-            for i in range(per):
+            for i, m in enumerate(pairs[first:first + per]):
                 for j in (range(2) if part is None else (part,)):
                     at = j * sub if part is None else 0
-                    half[2 * (first + i) + j, pl.ds(0, rows), :] = product[
+                    half[2 * m + j, pl.ds(0, rows), :] = product[
                         i * rows:(i + 1) * rows, at:at + sub]
 
     def mix_step(section, start, rows, inner, goal=None):
@@ -186,8 +188,9 @@
             return out_ref.at[span, pl.ds(pl.multiple_of(blk * wide, sub), wide)]
         return recv.at[section, blk, span, :]
 
-    def push(section, chunk, target, inner=None):
-        span = pl.ds(starts[chunk], sizes[chunk])
+    def push(section, chunk, target, inner=None, rows=None):
+        first, count = (0, sizes[chunk]) if rows is None else rows
+        span = pl.ds(starts[chunk] + first, count)
         source, goal = send.at[section, target, span, :], place(section, span)
         if inner is not None:
             source, goal = (ref.at[:, pl.ds(inner * sub, sub)] for ref in (source, goal))
@@ -200,68 +203,109 @@
         pltpu.make_async_copy(
             send.at[section, blk, span, :], place(section, span), recv_sem.at[section, chunk]).start()
 
-    def push_some(section, chunk, first, last, inner=None):
+    def push_some(section, chunk, first, last, inner=None, rows=None):
         @pl.loop(first, last)
         def _(target):
-            push(section, chunk, target, inner)
+            push(section, chunk, target, inner, rows)
 
     def push_all(section, chunk, inner=None):
-        for step in range(1, blocks):
-            push(section, chunk, lax.rem(blk + step, blocks), inner)
-
-    def meet(of_near, of_far):
-        if of_near:
-            @pl.when(blk < far - 1)
-            def _():
-                pl.semaphore_wait(near_sem, far - 1 - blk)
-        if of_far:
-            @pl.when(blk < blocks - 1)
-            def _():
-                pl.semaphore_wait(far_sem, blocks - lax.max(far, blk + 1))
+        base = blk // middle * middle
+        side = lax.rem(blk, 4) // 2 * 2
+        for step in range(1, middle):
+            push(section, chunk, base + lax.rem(blk - base + step, middle), inner)
+        for step in range(middle):
+            plane, at = step // 4 * 4, step % 4
+            push(section, chunk, lax.rem(base + middle, blocks) + plane + lax.rem(side + 2 + at, 4), inner)
+
+    stages = [(i, (2 * i, 2 * i + 1)) for i in range(low // 2)] if split else [(None, range(low))]
+
+    def push_first(inner, rows=None):
+        push_some(0, 0, 0, blk, inner, rows)
+
+        @pl.loop(blk + 1, blocks)
+        def _(target):
+            if inner == 0:
+                pl.semaphore_wait(go_sem.at[target], 1)
+            push(0, 0, target, inner, rows)
+
+    def tell_lender():
+        pl.semaphore_signal(all_sem, inc=1, device_id={"grp": 0}, device_id_type=MESH)
+
+    def enter():
+        pl.semaphore_wait(barrier, blk + groups - 1)
+        send_mix()
+
+    def announce():
+        @pl.loop(0, blk)
+        def _(other):
+            pl.semaphore_signal(go_sem.at[blk], inc=1, device_id={"blk": other}, device_id_type=MESH)
 
     def first_chunk():
         start, rows = starts[0], sizes[0]
-        load(0).wait()
+        own_mixing()
 
         @pl.when(grp == 0)
         def _():
-            leaf_step(0, start, rows)
-            for l in range(low):
-                if l > 0:
+            own_leaf.wait()
+            load(0).wait()
+            for stage, inner in stages:
+                leaf_step(0, start, rows, None, stage)
+                for l in inner:
                     build_weights(0, [l])
-                mix_step(0, start, rows, [l])
-                push_some(0, 0, 0, blk, l)
+                    mix_step(0, start, rows, [l])
+                    if l == 0:
+                        enter()
+                        for part in range(2):
+                            send_leaf(part)
+                        announce()
+                    push_some(0, 0, 0, blk, l)
             keep(0, 0)
-            meet(True, False)
-            push_some(0, 0, blk + 1, far)
-            meet(False, True)
-            push_some(0, 0, lax.max(far, blk + 1), blocks)
+
+            @pl.loop(blk + 1, blocks)
+            def _(target):
+                pl.semaphore_wait(go_sem.at[target], 1)
+                push(0, 0, target)
 
         @pl.when(grp > 0)
         def _():
+            enter()
+            announce()
+            if lend:
+                pl.when(blk >= middle)(tell_lender)
+            own_leaf.wait()
+            for part in range(2):
+                send_leaf(part)
+            mix_copy(0, 0).wait_recv()
+            build_weights(0, range(low))
+            load(0).wait()
 
             def share(l):
                 mix_step(0, start, rows, [l])
                 if lend and l == given:
                     def rest(first, last):
-                        push_some(0, 0, 0, lax.min(blk, first), l)
-                        push_some(0, 0, blk + 1, first, l)
-                        push_some(0, 0, last, blk, l)
-                        push_some(0, 0, lax.max(last, blk + 1), blocks, l)
+                        part = (0, lent_rows)
+                        push_some(0, 0, 0, lax.min(blk, first), l, part)
+                        push_some(0, 0, blk + 1, first, l, part)
+                        push_some(0, 0, last, blk, l, part)
+                        push_some(0, 0, lax.max(last, blk + 1), blocks, l, part)
+                    if rows > lent_rows:
+                        push_first(l, (lent_rows, rows - lent_rows))
                     each_half(rest)
                 else:
-                    push_all(0, 0, l)
-
-            meet(True, True)
-            if lend:
-                pl.semaphore_signal(all_sem, inc=1, device_id={"grp": 0}, device_id_type=MESH)
-            for part in range(2):
-                leaf_copy(0, 0, part).wait_recv()
-                leaf_step(0, start, rows, part)
-                if split:
-                    for l in range(part, low, 2):
-                        share(l)
-            if not split:
+                    push_first(l)
+                if lend and l == 0:
+                    pl.when(blk < middle)(tell_lender)
+
+            if split:
+                for part in range(2):
+                    leaf_copy(0, 0, part).wait_recv()
+                    for stage, inner in stages:
+                        leaf_step(0, start, rows, part, stage)
+                        share(inner[part])
+            else:
+                for part in range(2):
+                    leaf_copy(0, 0, part).wait_recv()
+                leaf_step(0, start, rows)
                 for l in range(low):
                     share(l)
             keep(0, 0)
@@ -270,7 +314,7 @@
 
     def lent_copy(target):
         return pltpu.make_async_remote_copy(
-            lent.at[target], recv.at[0, blk, pl.ds(starts[0], sizes[0]), lent_cols],
+            lent.at[target], recv.at[0, blk, pl.ds(0, lent_rows), lent_cols],
             lent_sem, recv_sem.at[0, 0],
             device_id={"grp": 1, "blk": target}, device_id_type=MESH)
 
@@ -278,38 +322,14 @@
         @pl.when(grp == 0)
         def _():
             lent_load.wait()
-            leaf_step(0, own_cols, sizes[0], given % 2)
-            mix_step(0, own_cols, sizes[0], [given], lent)
+            leaf_step(0, own_cols, lent_rows, given % 2)
+            mix_step(0, own_cols, lent_rows, [given], lent)
             pl.semaphore_wait(all_sem, 1)
 
             def start(first, last):
                 for step in range(last - first):
                     lent_copy(first + lax.rem(blk + step, last - first)).start()
             each_half(start)
-
-    own_mixing()
-
-    @pl.when(grp == 0)
-    def _():
-        build_weights(0, [0])
-
-    pl.semaphore_wait(barrier, blk + groups - 1)
-    send_factors()
-
-    @pl.loop(0, blk)
-    def _(other):
-        @pl.when(blk < far)
-        def _():
-            pl.semaphore_signal(near_sem, inc=1, device_id={"blk": other}, device_id_type=MESH)
-
-        @pl.when(blk >= far)
-        def _():
-            pl.semaphore_signal(far_sem, inc=1, device_id={"blk": other}, device_id_type=MESH)
-
-    @pl.when(grp > 0)
-    def _():
-        mix_copy(0, 0).wait_recv()
-        build_weights(0, range(low))
 
     for section in range(groups):
         if section > 0:
@@ -370,8 +390,12 @@
                 def _():
                     def sent(first, last):
                         whole = left.at[:, :, pl.ds(0, given * sub)]
-                        part = left.at[pl.ds(0, blocks - 1 - (last - first)), :, lent_cols]
-                        for piece in (whole, part):
+                        part = left.at[
+                            pl.ds(0, blocks - 1 - (last - first)), pl.ds(0, lent_rows), lent_cols]
+                        pieces = [whole, part]
+                        if rows > lent_rows:
+                            pieces.append(left.at[:, pl.ds(lent_rows, rows - lent_rows), lent_cols])
+                        for piece in pieces:
                             pltpu.make_async_copy(piece, piece, send_sem.at[section, chunk]).wait()
                     each_half(sent)
             else:
@@ -401,7 +425,7 @@
         in_specs=[in_hbm, in_hbm, in_hbm],
         out_specs=pl.BlockSpec(memory_space=pl.ANY),
         scratch_shapes=[
-            pltpu.VMEM((own_cols + sizes[0], rows_dev), bf16),
+            pltpu.VMEM((own_cols + TILE, rows_dev), bf16),
             pltpu.VMEM((groups, blocks, own_cols, low * sub), bf16),
             pltpu.VMEM((groups - 1, blocks, own_cols, low * sub), bf16),
             pltpu.VMEM((leaves, 2 * TILE, sub), bf16),
@@ -409,13 +433,13 @@
             pltpu.VMEM((low, blocks, blocks), bf16),
             pltpu.VMEM((groups, blocks, width), bf16),
             pltpu.VMEM((low, big, big), bf16),
-            pltpu.VMEM((blocks, sizes[0], sub), bf16),
+            pltpu.VMEM((blocks, TILE, sub), bf16),
             dma((len(sizes) + 1,)),
             dma((groups, len(sizes))),
             dma((groups, len(sizes))),
             dma((2,)),
             dma((groups, 2)), dma((groups, 2)), dma((groups,)), dma((groups,)), dma,
-            pltpu.SemaphoreType.REGULAR, pltpu.SemaphoreType.REGULAR, pltpu.SemaphoreType.REGULAR,
+            pltpu.SemaphoreType.REGULAR((blocks,)), pltpu.SemaphoreType.REGULAR,
         ],
         compiler_params=pltpu.CompilerParams(
             collective_id=0, has_side_effects=True, vmem_limit_bytes=48 * 1024 * 1024),

time: 97.9 us -> 98.1 us (level)
  no operation moved by 1% of the time
where the time goes in v3:
time: 98.1 us; the launch traced here: 97.7 us
  Pallas kernels  96.3 us (98%)
  local copies, waits for them, and re-layouts  1.32 us (1%)
    pallas_call x1, Pallas kernels, on_device(): pl.pallas_call(functools.partial(chain_kernel, groups, blocks, own_cols,...  96.3 us

profile of v3, /device:TPU:15, one launch (start us, length us, event | category | flops | bytes accessed | tf_op | source)
XLA Modules:
  0.0 97.7 jit_solution(17742853602753291899)
XLA Ops:
  0.0 96.3 %shard_map.37 = bf16[128,8192]{1,0:T(8,128)(2,1)S(1)} custom-call(bf16[256,8192]{1,0:T(8,128)(2,1)} %sketch_ref.1, bf16[1,1,256,256]{3,2,1,0:T(8,128)(2,1)} %leaf_in.1, bf16[1,4,16,16]{3,2,1,0:T(8,128)(2,1)} %mix_in.1), custom_call_target="tpu_custom_call" | custom-call | tf_op jit(solution)/shard_map/pallas_call | solution.py:422
  96.3 1.3 %copy.5 = bf16[128,8192]{1,0:T(8,128)(2,1)} copy(bf16[128,8192]{1,0:T(8,128)(2,1)S(1)} %shard_map.37) | data formatting | bytes 4194304

commit v4 on v3

--- a/solution.py
+++ b/solution.py
@@ -28,7 +28,7 @@
 def chain_kernel(
     groups, blocks, own_cols, sizes, sketch_ref, leaf_in, mix_in, out_ref,
     x_vm, send, recv, half, leaf_all, mix_vm, mix_all, weights, lent,
-    x_sem, send_sem, recv_sem, own_sem, leaf_send, leaf_recv, mix_send, mix_recv, lent_sem,
+    x_sem, sent_sem, recv_sem, own_sem, leaf_recv, mix_recv,
     go_sem, all_sem,
 ):
     grp = lax.axis_index("grp")
@@ -49,7 +49,8 @@
     lent_rows = lent.shape[1]
     given = low - 1
     middle = blocks // 2
-    lent_to = ((blocks - middle // 4, blocks), (0, middle // 2))
+    pair = 2 - blocks % 2
+    lent_to = ((blocks - middle // 4, blocks), (0, middle * 3 // 4))
 
     def each_half(act):
         for upper in range(2):
@@ -89,13 +90,13 @@
 
     def mix_copy(target, owner):
         return pltpu.make_async_remote_copy(
-            mix_all.at[owner], mix_all.at[owner], mix_send.at[target], mix_recv.at[owner],
+            mix_all.at[owner], mix_all.at[owner], sent_sem, mix_recv.at[owner],
             device_id={"grp": target}, device_id_type=MESH)
 
     def leaf_copy(target, owner, part):
         return pltpu.make_async_remote_copy(
             leaf_all.at[owner, :, parts[part]], leaf_all.at[owner, :, parts[part]],
-            leaf_send.at[target, part], leaf_recv.at[owner, part],
+            sent_sem, leaf_recv.at[owner, part],
             device_id={"grp": target}, device_id_type=MESH)
 
     def send_mix():
@@ -195,7 +196,7 @@
         if inner is not None:
             source, goal = (ref.at[:, pl.ds(inner * sub, sub)] for ref in (source, goal))
         pltpu.make_async_remote_copy(
-            source, goal, send_sem.at[section, chunk], recv_sem.at[section, chunk],
+            source, goal, sent_sem, recv_sem.at[section, chunk],
             device_id={"blk": target}, device_id_type=MESH).start()
 
     def keep(section, chunk):
@@ -219,14 +220,23 @@
 
     stages = [(i, (2 * i, 2 * i + 1)) for i in range(low // 2)] if split else [(None, range(low))]
 
+    def push_upper(inner=None, rows=None, meet=True):
+        @pl.when(lax.rem(blk, pair) < pair - 1)
+        def _():
+            if meet:
+                pl.semaphore_wait(go_sem.at[blk // pair], 1)
+            push(0, 0, blk + 1, inner, rows)
+
+        @pl.loop(blk // pair + 1, blocks // pair)
+        def _(group):
+            if meet:
+                pl.semaphore_wait(go_sem.at[group], pair)
+            for member in range(pair):
+                push(0, 0, group * pair + member, inner, rows)
+
     def push_first(inner, rows=None):
         push_some(0, 0, 0, blk, inner, rows)
-
-        @pl.loop(blk + 1, blocks)
-        def _(target):
-            if inner == 0:
-                pl.semaphore_wait(go_sem.at[target], 1)
-            push(0, 0, target, inner, rows)
+        push_upper(inner, rows, inner == 0)
 
     def tell_lender():
         pl.semaphore_signal(all_sem, inc=1, device_id={"grp": 0}, device_id_type=MESH)
@@ -238,7 +248,8 @@
     def announce():
         @pl.loop(0, blk)
         def _(other):
-            pl.semaphore_signal(go_sem.at[blk], inc=1, device_id={"blk": other}, device_id_type=MESH)
+            pl.semaphore_signal(
+                go_sem.at[blk // pair], inc=1, device_id={"blk": other}, device_id_type=MESH)
 
     def first_chunk():
         start, rows = starts[0], sizes[0]
@@ -246,25 +257,23 @@
 
         @pl.when(grp == 0)
         def _():
+            build_weights(0, [0])
             own_leaf.wait()
+            enter()
+            for part in range(2):
+                send_leaf(part)
+            announce()
             load(0).wait()
             for stage, inner in stages:
                 leaf_step(0, start, rows, None, stage)
                 for l in inner:
-                    build_weights(0, [l])
+                    if l > 0:
+                        build_weights(0, [l])
                     mix_step(0, start, rows, [l])
-                    if l == 0:
-                        enter()
-                        for part in range(2):
-                            send_leaf(part)
-                        announce()
                     push_some(0, 0, 0, blk, l)
             keep(0, 0)
 
-            @pl.loop(blk + 1, blocks)
-            def _(target):
-                pl.semaphore_wait(go_sem.at[target], 1)
-                push(0, 0, target)
+            push_upper()
 
         @pl.when(grp > 0)
         def _():
@@ -315,7 +324,7 @@
     def lent_copy(target):
         return pltpu.make_async_remote_copy(
             lent.at[target], recv.at[0, blk, pl.ds(0, lent_rows), lent_cols],
-            lent_sem, recv_sem.at[0, 0],
+            sent_sem, recv_sem.at[0, 0],
             device_id={"grp": 1, "blk": target}, device_id_type=MESH)
 
     def lent_chunk():
@@ -367,40 +376,30 @@
             if section == 0 and chunk == 1 and lend:
                 lent_chunk()
 
+    def drain(*parts):
+        for part in parts:
+            pltpu.make_async_copy(part, part, sent_sem).wait()
+
     for step in range(1, groups):
-        target = lax.rem(grp + step, groups)
-        mix_copy(target, grp).wait_send()
-        for part in range(2):
-            leaf_copy(target, grp, part).wait_send()
+        drain(mix_all.at[grp], leaf_all.at[grp])
+    left = send.at[:, pl.ds(0, blocks - 1)]
+    if lend:
+        @pl.when(grp == 0)
+        def _():
+            drain(left)
+            each_half(lambda first, last: drain(lent.at[pl.ds(0, last - first)]))
+
+        @pl.when(grp > 0)
+        def _():
+            top, under = pl.ds(0, lent_rows), pl.ds(lent_rows, own_cols - lent_rows)
+            drain(left.at[pl.ds(1, groups - 1)], left.at[0, :, under], left.at[
+                0, :, top, pl.ds(0, given * sub)])
+            each_half(lambda first, last: drain(
+                left.at[0, pl.ds(0, blocks - 1 - (last - first)), top, lent_cols]))
+    else:
+        drain(left)
     for chunk, (start, rows) in enumerate(zip(starts, sizes)):
-        span = pl.ds(start, rows)
-        for section in range(groups):
-            left = send.at[section, pl.ds(0, blocks - 1), span, :]
-            if lend and section == 0 and chunk == 0:
-                @pl.when(grp == 0)
-                def _():
-                    pltpu.make_async_copy(left, left, send_sem.at[section, chunk]).wait()
-
-                    def sent(first, last):
-                        part = lent.at[pl.ds(0, last - first)]
-                        pltpu.make_async_copy(part, part, lent_sem).wait()
-                    each_half(sent)
-
-                @pl.when(grp > 0)
-                def _():
-                    def sent(first, last):
-                        whole = left.at[:, :, pl.ds(0, given * sub)]
-                        part = left.at[
-                            pl.ds(0, blocks - 1 - (last - first)), pl.ds(0, lent_rows), lent_cols]
-                        pieces = [whole, part]
-                        if rows > lent_rows:
-                            pieces.append(left.at[:, pl.ds(lent_rows, rows - lent_rows), lent_cols])
-                        for piece in pieces:
-                            pltpu.make_async_copy(piece, piece, send_sem.at[section, chunk]).wait()
-                    each_half(sent)
-            else:
-                pltpu.make_async_copy(left, left, send_sem.at[section, chunk]).wait()
-        arrived = out_ref.at[span, :]
+        arrived = out_ref.at[pl.ds(start, rows), :]
         pltpu.make_async_copy(arrived, arrived, recv_sem.at[groups - 1, chunk]).wait()
 
 
@@ -435,11 +434,10 @@
             pltpu.VMEM((low, big, big), bf16),
             pltpu.VMEM((blocks, TILE, sub), bf16),
             dma((len(sizes) + 1,)),
+            dma,
             dma((groups, len(sizes))),
-            dma((groups, len(sizes))),
-            dma((2,)),
-            dma((groups, 2)), dma((groups, 2)), dma((groups,)), dma((groups,)), dma,
-            pltpu.SemaphoreType.REGULAR((blocks,)), pltpu.SemaphoreType.REGULAR,
+            dma((2,)), dma((groups, 2)), dma((groups,)),
+            pltpu.SemaphoreType.REGULAR((blocks // (2 - blocks % 2),)), pltpu.SemaphoreType.REGULAR,
         ],
         compiler_params=pltpu.CompilerParams(
             collective_id=0, has_side_effects=True, vmem_limit_bytes=48 * 1024 * 1024),

time: 98.1 us -> 97.6 us (level)
  Pallas kernels: 96.3 us -> 95.3 us
    pallas_call x1, Pallas kernels: 96.3 us -> 95.3 us  [on_device(): pl.pallas_call(functools.partial(chain_kernel, groups, blocks, own_cols,...]
where the time goes in v4:
time: 97.6 us; the launch traced here: 96.6 us
  Pallas kernels  95.3 us (98%)
  local copies, waits for them, and re-layouts  1.32 us (1%)
    pallas_call x1, Pallas kernels, on_device(): pl.pallas_call(functools.partial(chain_kernel, groups, blocks, own_cols,...  95.3 us

profile of v4, /device:TPU:15, one launch (start us, length us, event | category | flops | bytes accessed | tf_op | source)
XLA Modules:
  0.0 96.6 jit_solution(6338524853103208683)
XLA Ops:
  0.0 95.3 %shard_map.37 = bf16[128,8192]{1,0:T(8,128)(2,1)S(1)} custom-call(bf16[256,8192]{1,0:T(8,128)(2,1)} %sketch_ref.1, bf16[1,1,256,256]{3,2,1,0:T(8,128)(2,1)} %leaf_in.1, bf16[1,4,16,16]{3,2,1,0:T(8,128)(2,1)} %mix_in.1), custom_call_target="tpu_custom_call" | custom-call | tf_op jit(solution)/shard_map/pallas_call | solution.py:421
  95.3 1.3 %copy.5 = bf16[128,8192]{1,0:T(8,128)(2,1)} copy(bf16[128,8192]{1,0:T(8,128)(2,1)S(1)} %shard_map.37) | data formatting | bytes 4194304

commit v5 on v4

--- a/solution.py
+++ b/solution.py
@@ -209,14 +209,24 @@
         def _(target):
             push(section, chunk, target, inner, rows)
 
-    def push_all(section, chunk, inner=None):
+    def push_all(section, chunk):
         base = blk // middle * middle
+        opposite = lax.rem(base + middle, blocks)
+        for step in range(1, middle):
+            push(section, chunk, base + lax.rem(blk - base + step, middle))
+        if middle % 4:
+            for step in range(middle):
+                push(section, chunk, opposite + step)
+            return
         side = lax.rem(blk, 4) // 2 * 2
-        for step in range(1, middle):
-            push(section, chunk, base + lax.rem(blk - base + step, middle), inner)
-        for step in range(middle):
-            plane, at = step // 4 * 4, step % 4
-            push(section, chunk, lax.rem(base + middle, blocks) + plane + lax.rem(side + 2 + at, 4), inner)
+        lower = (blk < middle).astype(jnp.int32)
+        spots = [(plane, at) for plane in range(middle // 4) for at in range(4)]
+        rising = sorted(spots, key=lambda spot: (spot[1], spot[0]))
+        falling = sorted(spots, key=lambda spot: (spot[0] * 2 + spot[1], spot[0]))
+        for (plane, at), (other_plane, other_at) in zip(rising, falling):
+            plane = lower * plane + (1 - lower) * other_plane
+            at = lower * (at ^ 1) + (1 - lower) * (other_at ^ 1)
+            push(section, chunk, opposite + plane * 4 + lax.rem(side + 2 + at, 4))
 
     stages = [(i, (2 * i, 2 * i + 1)) for i in range(low // 2)] if split else [(None, range(low))]
 
@@ -264,13 +274,23 @@
                 send_leaf(part)
             announce()
             load(0).wait()
-            for stage, inner in stages:
-                leaf_step(0, start, rows, None, stage)
-                for l in inner:
-                    if l > 0:
-                        build_weights(0, [l])
-                    mix_step(0, start, rows, [l])
-                    push_some(0, 0, 0, blk, l)
+
+            @pl.when(blk >= middle)
+            def _():
+                for stage, inner in stages:
+                    leaf_step(0, start, rows, None, stage)
+                    for l in inner:
+                        if l > 0:
+                            build_weights(0, [l])
+                        mix_step(0, start, rows, [l])
+                        push_some(0, 0, 0, blk, l)
+
+            @pl.when(blk < middle)
+            def _():
+                build_weights(0, range(1, low))
+                compute(0, start, rows)
+                push_some(0, 0, 0, blk)
+
             keep(0, 0)
 
             push_upper()

time: 97.6 us -> 97.2 us (level)
  no operation moved by 1% of the time
where the time goes in v5:
time: 97.2 us; the launch traced here: 95.9 us
  Pallas kernels  94.6 us (97%)
  local copies, waits for them, and re-layouts  1.32 us (1%)
    pallas_call x1, Pallas kernels, on_device(): pl.pallas_call(functools.partial(chain_kernel, groups, blocks, own_cols,...  94.6 us

profile of v5, /device:TPU:15, one launch (start us, length us, event | category | flops | bytes accessed | tf_op | source)
XLA Modules:
  0.0 95.9 jit_solution(3732035901463279391)
XLA Ops:
  0.0 94.6 %shard_map.37 = bf16[128,8192]{1,0:T(8,128)(2,1)S(1)} custom-call(bf16[256,8192]{1,0:T(8,128)(2,1)} %sketch_ref.1, bf16[1,1,256,256]{3,2,1,0:T(8,128)(2,1)} %leaf_in.1, bf16[1,4,16,16]{3,2,1,0:T(8,128)(2,1)} %mix_in.1), custom_call_target="tpu_custom_call" | custom-call | tf_op jit(solution)/shard_map/pallas_call | solution.py:441
  94.6 1.3 %copy.5 = bf16[128,8192]{1,0:T(8,128)(2,1)} copy(bf16[128,8192]{1,0:T(8,128)(2,1)S(1)} %shard_map.37) | data formatting | bytes 4194304

commit v6 on v5

--- a/solution.py
+++ b/solution.py
@@ -28,7 +28,7 @@
 def chain_kernel(
     groups, blocks, own_cols, sizes, sketch_ref, leaf_in, mix_in, out_ref,
     x_vm, send, recv, half, leaf_all, mix_vm, mix_all, weights, lent,
-    x_sem, sent_sem, recv_sem, own_sem, leaf_recv, mix_recv,
+    x_sem, sent_sem, recv_sem, last_sem, own_sem, leaf_recv, mix_recv,
     go_sem, all_sem,
 ):
     grp = lax.axis_index("grp")
@@ -189,6 +189,9 @@
             return out_ref.at[span, pl.ds(pl.multiple_of(blk * wide, sub), wide)]
         return recv.at[section, blk, span, :]
 
+    def landed(section, chunk):
+        return last_sem if section == groups - 1 else recv_sem.at[section, chunk]
+
     def push(section, chunk, target, inner=None, rows=None):
         first, count = (0, sizes[chunk]) if rows is None else rows
         span = pl.ds(starts[chunk] + first, count)
@@ -196,13 +199,13 @@
         if inner is not None:
             source, goal = (ref.at[:, pl.ds(inner * sub, sub)] for ref in (source, goal))
         pltpu.make_async_remote_copy(
-            source, goal, sent_sem, recv_sem.at[section, chunk],
+            source, goal, sent_sem, landed(section, chunk),
             device_id={"blk": target}, device_id_type=MESH).start()
 
     def keep(section, chunk):
         span = pl.ds(starts[chunk], sizes[chunk])
         pltpu.make_async_copy(
-            send.at[section, blk, span, :], place(section, span), recv_sem.at[section, chunk]).start()
+            send.at[section, blk, span, :], place(section, span), landed(section, chunk)).start()
 
     def push_some(section, chunk, first, last, inner=None, rows=None):
         @pl.loop(first, last)
@@ -418,9 +421,7 @@
                 left.at[0, pl.ds(0, blocks - 1 - (last - first)), top, lent_cols]))
     else:
         drain(left)
-    for chunk, (start, rows) in enumerate(zip(starts, sizes)):
-        arrived = out_ref.at[pl.ds(start, rows), :]
-        pltpu.make_async_copy(arrived, arrived, recv_sem.at[groups - 1, chunk]).wait()
+    pltpu.make_async_copy(out_ref, out_ref, last_sem).wait()
 
 
 def on_device(sketch, leaf_maps, mix_maps):
@@ -455,7 +456,8 @@
             pltpu.VMEM((blocks, TILE, sub), bf16),
             dma((len(sizes) + 1,)),
             dma,
-            dma((groups, len(sizes))),
+            dma((groups - 1, len(sizes))),
+            dma,
             dma((2,)), dma((groups, 2)), dma((groups,)),
             pltpu.SemaphoreType.REGULAR((blocks // (2 - blocks % 2),)), pltpu.SemaphoreType.REGULAR,
         ],

time: 97.2 us -> 97.2 us (level)
  no operation moved by 1% of the time
where the time goes in v6:
time: 97.2 us; the launch traced here: 95.9 us
  Pallas kernels  94.6 us (97%)
  local copies, waits for them, and re-layouts  1.32 us (1%)
    pallas_call x1, Pallas kernels, on_device(): pl.pallas_call(functools.partial(chain_kernel, groups, blocks, own_cols,...  94.6 us

profile of v6, /device:TPU:15, one launch (start us, length us, event | category | flops | bytes accessed | tf_op | source)
XLA Modules:
  0.0 95.9 jit_solution(2067481915407543244)
XLA Ops:
  0.0 94.6 %shard_map.37 = bf16[128,8192]{1,0:T(8,128)(2,1)S(1)} custom-call(bf16[256,8192]{1,0:T(8,128)(2,1)} %sketch_ref.1, bf16[1,1,256,256]{3,2,1,0:T(8,128)(2,1)} %leaf_in.1, bf16[1,4,16,16]{3,2,1,0:T(8,128)(2,1)} %mix_in.1), custom_call_target="tpu_custom_call" | custom-call | tf_op jit(solution)/shard_map/pallas_call | solution.py:442
  94.6 1.3 %copy.5 = bf16[128,8192]{1,0:T(8,128)(2,1)} copy(bf16[128,8192]{1,0:T(8,128)(2,1)S(1)} %shard_map.37) | data formatting | bytes 4194304
